TPU v7x, 32 devices: a whole 2x2x4 slice. The times are simulated.
32 devices in a mesh: grp: 2 (over y), tok: 4 (over z), sec: 2 (over core), ch: 2 (over x).
Axes of the slice: x: 2, y: 2, z: 4, core: 2. Of those that a mesh axis runs over, the one named last changes fastest.
Arguments:
- features: bfloat16 [4096, 2048], P('ch', ('grp', 'tok', 'sec')), parts along dimension 1, may hold values from -6 to 6
- gate_one: bfloat16 [4096, 2048], P('ch', ('grp', 'tok', 'sec')), parts along dimension 1, may hold values from -6 to 6
- taps_one: bfloat16 [4096, 128], P('ch'), may hold values from -0.5 to 0.5
- long_filter: bfloat16 [4096, 1024], P('ch', ('tok', 'sec')), may hold values from -0.1875 to 0.1875
- skip_gain: float32 [4096], P('ch'), may hold values from 0.5 to 1.5
- taps_two: bfloat16 [4096, 128], P('ch'), may hold values from -0.5 to 0.5
- gate_two: bfloat16 [4096, 2048], P('ch', ('grp', 'tok', 'sec')), parts along dimension 1, may hold values from -6 to 6
Outputs:
- mixed_out: bfloat16 [4096, 2048], P('ch', ('grp', 'tok', 'sec')), parts along dimension 1
There are 2 independent parts, one for each index of `grp`. A program takes and returns all parts, laid end to end along the dimension named above; an argument that names none is the same for every part. Nothing has to cross between parts.
All inputs are finite; a program needn't handle non-finite values.
Results may differ from a plain program's by a relative error of at most 0.0057.
Values may be sent and summed in bfloat16 or wider, within the bound.
No kernel may reach another device: no remote copies, remote signals or barrier semaphores. Data moves between devices by JAX's collectives and lax.ppermute only.
A program may use at most 192 MiB of HBM per device.

v0:
```python
import math
import jax
import jax.numpy as jnp
from jax import lax
from jax.sharding import PartitionSpec as P


def passed_along(array, axis, by):
    length = lax.axis_size(axis)
    pairs = [(i, i + by) for i in range(length) if 0 <= i + by < length]
    return lax.ppermute(array, axis, pairs)


def depthwise(padded, kernel_taps):
    tap_count = kernel_taps.shape[1]
    length = padded.shape[1] - (tap_count - 1)
    group_size = 16
    total = jnp.zeros((padded.shape[0], length), jnp.float32)
    for first in range(0, tap_count, group_size):
        last = min(first + group_size, tap_count)
        stacked = jnp.stack(
            [padded[:, tap_count - 1 - k : tap_count - 1 - k + length] for k in range(first, last)],
            axis=1,
        )
        total = total + jnp.einsum(
            "cgl,cg->cl", stacked, kernel_taps[:, first:last], preferred_element_type=jnp.float32
        )
    return total


def angle_table(rows_count, cols_count, period):
    row_index = jnp.arange(rows_count, dtype=jnp.int32)[:, None]
    col_index = jnp.arange(cols_count, dtype=jnp.int32)[None, :]
    phase = (row_index * col_index % period).astype(jnp.float32) * (2.0 * math.pi / period)
    return (jnp.cos(phase), jnp.sin(phase))


def contract(form, left, right):
    return jnp.einsum(form, left, right, precision=lax.Precision.HIGHEST)


def forward_spectrum(signal, outer, inner, total):
    half_outer = outer // 2
    cos_first, sin_first = angle_table(half_outer, outer, outer)
    turn_cos, turn_sin = angle_table(outer, inner, total)
    cos_inner, sin_inner = angle_table(inner, inner, inner)
    shaped = signal.reshape(signal.shape[0], half_outer, inner)
    real_a = contract("cmn,mk->ckn", shaped, cos_first)
    imag_a = -contract("cmn,mk->ckn", shaped, sin_first)
    real_b = real_a * turn_cos + imag_a * turn_sin
    imag_b = imag_a * turn_cos - real_a * turn_sin
    real_c = contract("ckn,nj->cjk", real_b, cos_inner) + contract("ckn,nj->cjk", imag_b, sin_inner)
    imag_c = contract("ckn,nj->cjk", imag_b, cos_inner) - contract("ckn,nj->cjk", real_b, sin_inner)
    return (real_c, imag_c)


def inverse_spectrum(real_y, imag_y, outer, inner, total):
    half_outer = outer // 2
    cos_inner, sin_inner = angle_table(inner, inner, inner)
    turn_cos, turn_sin = angle_table(outer, inner, total)
    cos_last, sin_last = angle_table(outer, half_outer, outer)
    real_c = contract("cjk,jn->ckn", real_y, cos_inner) - contract("cjk,jn->ckn", imag_y, sin_inner)
    imag_c = contract("cjk,jn->ckn", imag_y, cos_inner) + contract("cjk,jn->ckn", real_y, sin_inner)
    real_d = real_c * turn_cos - imag_c * turn_sin
    imag_d = imag_c * turn_cos + real_c * turn_sin
    result = contract("ckn,km->cmn", real_d, cos_last) - contract("ckn,km->cmn", imag_d, sin_last)
    return (result / total).reshape(real_y.shape[0], half_outer * inner)


def on_device(features, gate_one, taps_one, long_filter, skip_gain, taps_two, gate_two):
    shards = lax.axis_size(("tok", "sec"))
    channels, block_len = features.shape
    narrow = channels // shards
    seq_len = block_len * shards
    rim_width = taps_one.shape[1] - 1
    total = 2 * seq_len
    inner = math.gcd(seq_len, 128)
    outer = total // inner
    filter_rows = lax.all_to_all(
        long_filter[:, None, :], ("tok", "sec"), split_axis=0, concat_axis=1, tiled=True
    ).reshape(narrow, seq_len)
    rim_rows = passed_along(features[:, block_len - rim_width :], ("tok", "sec"), 1)
    first_conv = depthwise(jnp.concatenate([rim_rows, features], axis=1), taps_one)
    mixed_one = (first_conv * gate_one).astype(jnp.bfloat16)
    channel_rows = lax.all_to_all(
        mixed_one[:, None, :], ("tok", "sec"), split_axis=0, concat_axis=1, tiled=True
    )
    channel_rows = channel_rows.reshape(narrow, seq_len).astype(jnp.float32)
    filter_real, filter_imag = forward_spectrum(
        filter_rows.astype(jnp.float32), outer, inner, total
    )
    signal_real, signal_imag = forward_spectrum(channel_rows, outer, inner, total)
    product_real = signal_real * filter_real - signal_imag * filter_imag
    product_imag = signal_real * filter_imag + signal_imag * filter_real
    conv_rows = inverse_spectrum(product_real, product_imag, outer, inner, total)
    skip_local = lax.dynamic_slice_in_dim(
        skip_gain, lax.axis_index(("tok", "sec")) * narrow, narrow
    )
    long_out = (conv_rows + skip_local[:, None] * channel_rows).astype(jnp.bfloat16)
    long_blocks = long_out.reshape(narrow, shards, block_len)
    tail_rows = jnp.concatenate(
        [
            jnp.zeros((narrow, 1, rim_width), jnp.bfloat16),
            long_blocks[:, :-1, block_len - rim_width :],
        ],
        axis=1,
    )
    windows = jnp.concatenate([tail_rows, long_blocks], axis=2)
    padded = lax.all_to_all(
        windows, ("tok", "sec"), split_axis=1, concat_axis=0, tiled=True
    ).reshape(channels, block_len + rim_width)
    second_conv = depthwise(padded, taps_two)
    return (second_conv * gate_two).astype(jnp.bfloat16)


def solution(mesh):
    in_specs = (
        P("ch", ("grp", "tok", "sec")),
        P("ch", ("grp", "tok", "sec")),
        P("ch", None),
        P("ch", ("tok", "sec")),
        P("ch"),
        P("ch", None),
        P("ch", ("grp", "tok", "sec")),
    )
    out_specs = P("ch", ("grp", "tok", "sec"))
    return jax.shard_map(
        on_device, mesh=mesh, in_specs=in_specs, out_specs=out_specs, check_vma=False
    )
```

profile of v0, /device:TPU:0, one launch (start us, length us, event | category | flops | bytes accessed | tf_op | source)
XLA Modules:
  0.0 428.6 jit_solution(18028862349489927458)
XLA Ops:
  8.2 6.1 %all-to-all-start.1 = ((bf16[8,2,16384]{2,1,0:T(2,128)(2,1)}), bf16[8,2,16384]{2,1,0:T(2,128)(2,1)S(1)}, u32[]{:S(2)}, u32[]{:S(2)}) async-start(bf16[8,2,16384]{2,1,0:T(2,128)(2,1)} %reshape.112), calls=%async_computation.1 | async-start | bytes 1048576 | tf_op jit(solution)/shard_map/all_to_all | solution.py:79
  14.3 5.7 %slice_bitcast_fusion.142 = (bf16[2048,16,1]{1,0,2:T(8,128)(2,1)S(1)}, bf16[2048,16,1]{1,0,2:T(8,128)(2,1)}, bf16[2048,16,1]{1,0,2:T(8,128)(2,1)}, bf16[2048,16,...) fusion(bf16[2048,128]{1,0:T(8,128)(2,1)} %param.9), kind=kLoop, calls=%fused_computation.1013 | loop fusion | bytes 1048576 | tf_op jit(solution)/shard_map/slice | solution.py:26
  28.0 3.2 copy-done.13
  31.2 3.7 constant_dynamic-update-slice_fusion.16
  50.8 3.0 constant_dynamic-update-slice_fusion
  60.1 3.2 constant_dynamic-update-slice_fusion.32
  69.1 2.8 constant_dynamic-update-slice_fusion.48
  110.7 8.7 %fusion.16 = f32[2048,1,128]{2,1,0:T(1,128)S(1)} fusion(bf16[2048,16,128]{2,0,1:T(8,128)(2,1)} %constant_dynamic-update-slice_fusion.112, bf16[2048,16,1]{1,0,2:T(8,128)(2,1)S(1)} %get-tuple-element.191), kind=kOutput, calls=%fused_computation.268 | convolution fusion | flops 8388608 | bytes 9502720 | tf_op jit(solution)/shard_map/cgl,cg->cl/dot_general | solution.py:25
  119.4 8.7 %fusion.18 = f32[2048,1,128]{2,1,0:T(1,128)S(1)} fusion(bf16[2048,16,128]{2,0,1:T(8,128)(2,1)} %get-tuple-element.175, bf16[2048,16,1]{1,0,2:T(8,128)(2,1)S(1)} %get-tuple-element.192), kind=kOutput, calls=%fused_computation.270 | convolution fusion | flops 8388608 | bytes 9502720 | tf_op jit(solution)/shard_map/cgl,cg->cl/dot_general | solution.py:25
  128.2 9.0 %fusion.20 = f32[2048,1,128]{2,1,0:T(1,128)S(1)} fusion(bf16[2048,16,128]{2,0,1:T(8,128)(2,1)} %copy-done.9, bf16[2048,16,1]{1,0,2:T(8,128)(2,1)} %get-tuple-element.186), kind=kOutput, calls=%fused_computation.272 | convolution fusion | flops 8388608 | bytes 9502720 | tf_op jit(solution)/shard_map/cgl,cg->cl/dot_general | solution.py:25
  137.1 9.8 %fusion.22 = f32[2048,1,128]{2,1,0:T(1,128)} fusion(bf16[2048,16,128]{2,0,1:T(8,128)(2,1)} %copy-done.8, bf16[2048,16,1]{1,0,2:T(8,128)(2,1)} %get-tuple-element.187), kind=kOutput, calls=%fused_computation.274 | convolution fusion | flops 8388608 | bytes 9502720 | tf_op jit(solution)/shard_map/cgl,cg->cl/dot_general | solution.py:25
  146.9 10.2 %fusion.24 = f32[2048,1,128]{2,1,0:T(1,128)} fusion(bf16[2048,16,128]{2,0,1:T(8,128)(2,1)} %copy-done.7, bf16[2048,16,1]{1,0,2:T(8,128)(2,1)} %get-tuple-element.188), kind=kOutput, calls=%fused_computation.276 | convolution fusion | flops 8388608 | bytes 9502720 | tf_op jit(solution)/shard_map/cgl,cg->cl/dot_general | solution.py:25
  157.1 9.8 %fusion.26 = f32[2048,1,128]{2,1,0:T(1,128)} fusion(bf16[2048,16,128]{2,0,1:T(8,128)(2,1)} %copy-done.6, bf16[2048,16,1]{1,0,2:T(8,128)(2,1)} %get-tuple-element.189), kind=kOutput, calls=%fused_computation.278 | convolution fusion | flops 8388608 | bytes 9502720 | tf_op jit(solution)/shard_map/cgl,cg->cl/dot_general | solution.py:25
  166.8 9.9 %fusion.30 = f32[2048,1,128]{2,1,0:T(1,128)} fusion(bf16[2048,16,128]{2,0,1:T(8,128)(2,1)} %get-tuple-element.149, bf16[2048,16,1]{1,0,2:T(8,128)(2,1)S(1)} %get-tuple-element.190), kind=kOutput, calls=%fused_computation.282 | convolution fusion | flops 8388608 | bytes 9502720 | tf_op jit(solution)/shard_map/cgl,cg->cl/dot_general | solution.py:25
  176.7 9.8 %fusion.28 = f32[2048,1,128]{2,1,0:T(1,128)} fusion(bf16[2048,16,128]{2,0,1:T(8,128)(2,1)} %get-tuple-element.141, bf16[2048,16,1]{1,0,2:T(8,128)(2,1)S(1)} %get-tuple-element.185), kind=kOutput, calls=%fused_computation.280 | convolution fusion | flops 8388608 | bytes 9502720 | tf_op jit(solution)/shard_map/cgl,cg->cl/dot_general | solution.py:25
  186.5 2.9 fusion.111
  191.4 5.1 %all-to-all-start = ((bf16[8,2,16384]{2,1,0:T(2,128)(2,1)}), bf16[8,2,16384]{2,1,0:T(2,128)(2,1)}, u32[]{:S(2)}, u32[]{:S(2)}) async-start(bf16[8,2,16384]{2,1,0:T(2,128)(2,1)} %reshape.110), calls=%async_computation | async-start | bytes 1048576 | tf_op jit(solution)/shard_map/all_to_all | solution.py:85
  199.1 2.4 fusion.367
  201.5 10.4 %all-to-all-done = bf16[8,2,16384]{2,1,0:T(2,128)(2,1)} async-done(((bf16[8,2,16384]{2,1,0:T(2,128)(2,1)}), bf16[8,2,16384]{2,1,0:T(2,128)(2,1)}, u32[]{:S(2)}, u32[]{:S(2)}) %all-to-all-start) | async-done | bytes 524320 | tf_op jit(solution)/shard_map/all_to_all | solution.py:85
  211.9 2.6 reshape.111
  215.7 3.5 add_bitcast_fusion
  219.3 2.6 fusion.47
  221.9 2.6 fusion.45
  224.5 2.6 fusion.55
  227.1 2.7 fusion.53
  229.9 2.7 fusion.67
  232.6 2.7 fusion.70
  235.3 2.7 fusion.61
  238.0 3.3 multiply_subtract_fusion.1
  241.3 3.6 fusion.34
  244.9 3.6 fusion.32
  248.6 4.0 fusion.73
  252.5 3.8 multiply_subtract_fusion
  258.6 2.6 fusion.91
  263.2 3.7 all-to-all-start.2
  266.9 2.7 slice_bitcast_fusion.134
  269.6 23.6 %all-to-all-done.2 = bf16[256,8,255]{2,0,1:T(8,128)(2,1)S(1)} async-done(((bf16[256,8,255]{2,0,1:T(8,128)(2,1)}), bf16[256,8,255]{2,0,1:T(8,128)(2,1)S(1)}, u32[]{:S(2)}, u32[]{:S(2)}) %all-to-all-start.2) | async-done | bytes 1044512 | tf_op jit(solution)/shard_map/all_to_all | solution.py:109
  293.3 2.8 constant_dynamic-update-slice_fusion.159
  296.0 3.0 constant_dynamic-update-slice_fusion.158
  299.1 3.0 constant_dynamic-update-slice_fusion.157
  302.1 3.0 constant_dynamic-update-slice_fusion.156
  305.1 3.0 constant_dynamic-update-slice_fusion.155
  308.1 3.1 constant_dynamic-update-slice_fusion.154
  311.2 3.0 constant_dynamic-update-slice_fusion.153
  314.1 3.0 constant_dynamic-update-slice_fusion.152
  317.2 3.1 constant_dynamic-update-slice_fusion.151
  320.2 3.2 constant_dynamic-update-slice_fusion.150
  323.4 3.0 constant_dynamic-update-slice_fusion.149
  326.4 3.1 constant_dynamic-update-slice_fusion.148
  329.5 3.0 constant_dynamic-update-slice_fusion.147
  332.5 3.0 constant_dynamic-update-slice_fusion.146
  335.5 3.0 constant_dynamic-update-slice_fusion.145
  338.5 2.8 constant_dynamic-update-slice_fusion.144
  341.4 3.2 copy-done.10
  344.6 2.6 copy-done.11
  349.6 9.1 %fusion.14 = f32[2048,1,128]{2,1,0:T(1,128)S(1)} fusion(bf16[2048,16,128]{2,0,1:T(8,128)(2,1)} %get-tuple-element.20, bf16[2048,16,1]{1,0,2:T(8,128)(2,1)S(1)} %copy-done.5), kind=kOutput, calls=%fused_computation.266 | convolution fusion | flops 8388608 | bytes 9502720 | tf_op jit(solution)/shard_map/cgl,cg->cl/dot_general | solution.py:25
  358.7 8.7 %fusion.12 = f32[2048,1,128]{2,1,0:T(1,128)S(1)} fusion(bf16[2048,16,128]{2,0,1:T(8,128)(2,1)} %copy-done.10, bf16[2048,16,1]{1,0,2:T(8,128)(2,1)S(1)} %copy-done.4), kind=kOutput, calls=%fused_computation.264 | convolution fusion | flops 8388608 | bytes 9502720 | tf_op jit(solution)/shard_map/cgl,cg->cl/dot_general | solution.py:25
  367.5 8.9 %fusion.10 = f32[2048,1,128]{2,1,0:T(1,128)S(1)} fusion(bf16[2048,16,128]{2,0,1:T(8,128)(2,1)} %get-tuple-element.19, bf16[2048,16,1]{1,0,2:T(8,128)(2,1)S(1)} %get-tuple-element.181), kind=kOutput, calls=%fused_computation.262 | convolution fusion | flops 8388608 | bytes 9502720 | tf_op jit(solution)/shard_map/cgl,cg->cl/dot_general | solution.py:25
  376.4 8.8 %fusion.8 = f32[2048,1,128]{2,1,0:T(1,128)S(1)} fusion(bf16[2048,16,128]{2,0,1:T(8,128)(2,1)} %get-tuple-element.18, bf16[2048,16,1]{1,0,2:T(8,128)(2,1)} %get-tuple-element.180), kind=kOutput, calls=%fused_computation.260 | convolution fusion | flops 8388608 | bytes 9502720 | tf_op jit(solution)/shard_map/cgl,cg->cl/dot_general | solution.py:25
  385.1 9.9 %fusion.6 = f32[2048,1,128]{2,1,0:T(1,128)} fusion(bf16[2048,16,128]{2,0,1:T(8,128)(2,1)} %get-tuple-element.17, bf16[2048,16,1]{1,0,2:T(8,128)(2,1)} %get-tuple-element.179), kind=kOutput, calls=%fused_computation.258 | convolution fusion | flops 8388608 | bytes 9502720 | tf_op jit(solution)/shard_map/cgl,cg->cl/dot_general | solution.py:25
  395.0 9.8 %fusion.4 = f32[2048,1,128]{2,1,0:T(1,128)} fusion(bf16[2048,16,128]{2,0,1:T(8,128)(2,1)} %get-tuple-element.16, bf16[2048,16,1]{1,0,2:T(8,128)(2,1)} %get-tuple-element.178), kind=kOutput, calls=%fused_computation.256 | convolution fusion | flops 8388608 | bytes 9502720 | tf_op jit(solution)/shard_map/cgl,cg->cl/dot_general | solution.py:25
  404.8 9.7 %fusion.2 = f32[2048,1,128]{2,1,0:T(1,128)} fusion(bf16[2048,16,128]{2,0,1:T(8,128)(2,1)} %copy-done.12, bf16[2048,16,1]{1,0,2:T(8,128)(2,1)S(1)} %get-tuple-element.184), kind=kOutput, calls=%fused_computation.254 | convolution fusion | flops 8388608 | bytes 9502720 | tf_op jit(solution)/shard_map/cgl,cg->cl/dot_general | solution.py:25
  414.5 10.1 %fusion = f32[2048,1,128]{2,1,0:T(1,128)} fusion(bf16[2048,16,128]{2,0,1:T(8,128)(2,1)} %copy-done.11, bf16[2048,16,1]{1,0,2:T(8,128)(2,1)} %get-tuple-element.183), kind=kOutput, calls=%fused_computation.252 | convolution fusion | flops 8388608 | bytes 9502720 | tf_op jit(solution)/shard_map/cgl,cg->cl/dot_general | solution.py:25
  424.5 3.6 multiply_convert_fusion
  (140 shorter events, 95.1 us)
Async XLA Ops:
  0.0 20.0 %copy-start = (bf16[2048,128]{1,0:T(8,128)(2,1)S(1)}, bf16[2048,128]{1,0:T(8,128)(2,1)}, u32[]{:S(2)}) copy-start(bf16[2048,128]{1,0:T(8,128)(2,1)} %param.7) | copy-start | bytes 1572868
  2.1 17.9 %collective-permute-start = (bf16[2048,127]{1,0:T(8,128)(2,1)}, bf16[2048,127]{1,0:T(8,128)(2,1)S(1)}, u32[]{:S(2)}, u32[]{:S(2)}) collective-permute-start(bf16[2048,127]{1,0:T(8,128)(2,1)} %slice.819), channel_id=1, source_target_pairs={{0,2},{2,4},{4,6},{6,8},{8,10},{10,12},{12,14},{1,3},{3,5},{5,7},{... | collective-permute-start | bytes 1560584 | tf_op jit(solution)/shard_map/ppermute | solution.py:11
  8.2 183.2 %all-to-all-start.1 = ((bf16[8,2,16384]{2,1,0:T(2,128)(2,1)}), bf16[8,2,16384]{2,1,0:T(2,128)(2,1)S(1)}, u32[]{:S(2)}, u32[]{:S(2)}) async-start(bf16[8,2,16384]{2,1,0:T(2,128)(2,1)} %reshape.112), calls=%async_computation.1 | async-start | bytes 1048576 | tf_op jit(solution)/shard_map/all_to_all | solution.py:79
  28.0 3.2 copy-start.13
  63.3 5.3 %copy-start.6 = (bf16[2048,16,128]{2,0,1:T(8,128)(2,1)}, bf16[2048,16,128]{2,0,1:T(8,128)(2,1)S(1)}, u32[]{:S(2)}) copy-start(bf16[2048,16,128]{2,0,1:T(8,128)(2,1)S(1)} %get-tuple-element.157) | copy-start | bytes 25165828
  71.9 5.3 %copy-start.7 = (bf16[2048,16,128]{2,0,1:T(8,128)(2,1)}, bf16[2048,16,128]{2,0,1:T(8,128)(2,1)S(1)}, u32[]{:S(2)}) copy-start(bf16[2048,16,128]{2,0,1:T(8,128)(2,1)S(1)} %get-tuple-element.163) | copy-start | bytes 25165828
  79.6 7.1 %copy-start.8 = (bf16[2048,16,128]{2,0,1:T(8,128)(2,1)}, bf16[2048,16,128]{2,0,1:T(8,128)(2,1)S(1)}, u32[]{:S(2)}) copy-start(bf16[2048,16,128]{2,0,1:T(8,128)(2,1)S(1)} %get-tuple-element.168) | copy-start | bytes 25165828
  86.7 14.3 %copy-start.9 = (bf16[2048,16,128]{2,0,1:T(8,128)(2,1)}, bf16[2048,16,128]{2,0,1:T(8,128)(2,1)S(1)}, u32[]{:S(2)}) copy-start(bf16[2048,16,128]{2,0,1:T(8,128)(2,1)S(1)} %get-tuple-element.172) | copy-start | bytes 25165828
  176.7 9.8 %copy-start.2 = (bf16[2048,128]{1,0:T(8,128)(2,1)S(1)}, bf16[2048,128]{1,0:T(8,128)(2,1)}, u32[]{:S(2)}) copy-start(bf16[2048,128]{1,0:T(8,128)(2,1)} %param.8) | copy-start | bytes 1572868
  191.4 20.5 %all-to-all-start = ((bf16[8,2,16384]{2,1,0:T(2,128)(2,1)}), bf16[8,2,16384]{2,1,0:T(2,128)(2,1)}, u32[]{:S(2)}, u32[]{:S(2)}) async-start(bf16[8,2,16384]{2,1,0:T(2,128)(2,1)} %reshape.110), calls=%async_computation | async-start | bytes 1048576 | tf_op jit(solution)/shard_map/all_to_all | solution.py:85
  256.3 10.6 %copy-start.1 = (bf16[2048,128]{1,0:T(8,128)(2,1)S(1)}, bf16[2048,128]{1,0:T(8,128)(2,1)}, u32[]{:S(2)}) copy-start(bf16[2048,128]{1,0:T(8,128)(2,1)} %param.12) | copy-start | bytes 1572868
  263.2 30.1 %all-to-all-start.2 = ((bf16[256,8,255]{2,0,1:T(8,128)(2,1)}), bf16[256,8,255]{2,0,1:T(8,128)(2,1)S(1)}, u32[]{:S(2)}, u32[]{:S(2)}) async-start(bf16[256,8,255]{2,0,1:T(8,128)(2,1)} %copy.106), calls=%async_computation.2 | async-start | bytes 2097152 | tf_op jit(solution)/shard_map/all_to_all | solution.py:109
  335.5 14.1 %copy-start.5 = (bf16[2048,16,1]{1,0,2:T(8,128)(2,1)S(1)}, bf16[2048,16,1]{1,0,2:T(8,128)(2,1)}, u32[]{:S(2)}) copy-start(bf16[2048,16,1]{1,0,2:T(8,128)(2,1)} %get-tuple-element.182) | copy-start | bytes 196612
  341.4 3.2 copy-start.10
  341.4 5.8 %copy-start.11 = (bf16[2048,16,128]{2,0,1:T(8,128)(2,1)}, bf16[2048,16,128]{2,0,1:T(8,128)(2,1)S(1)}, u32[]{:S(2)}) copy-start(bf16[2048,16,128]{2,0,1:T(8,128)(2,1)S(1)} %get-tuple-element.14) | copy-start | bytes 25165828
  341.4 8.2 %copy-start.12 = (bf16[2048,16,128]{2,0,1:T(8,128)(2,1)}, bf16[2048,16,128]{2,0,1:T(8,128)(2,1)S(1)}, u32[]{:S(2)}) copy-start(bf16[2048,16,128]{2,0,1:T(8,128)(2,1)S(1)} %get-tuple-element.15) | copy-start | bytes 25165828
  341.4 17.4 %copy-start.4 = (bf16[2048,16,1]{1,0,2:T(8,128)(2,1)S(1)}, bf16[2048,16,1]{1,0,2:T(8,128)(2,1)}, u32[]{:S(2)}) copy-start(bf16[2048,16,1]{1,0,2:T(8,128)(2,1)} %get-tuple-element.177) | copy-start | bytes 196612
  414.5 10.1 %copy-start.3 = (bf16[2048,128]{1,0:T(8,128)(2,1)S(1)}, bf16[2048,128]{1,0:T(8,128)(2,1)}, u32[]{:S(2)}) copy-start(bf16[2048,128]{1,0:T(8,128)(2,1)} %param.13) | copy-start | bytes 1572868
where the time goes:
time: 436 us; the launch traced here: 429 us
  matrix products  201 us (46%)
  other arithmetic  97.6 us (22%)
  local copies, waits for them, and re-layouts  78 us (18%)
  waiting for transfers between devices  34.1 us (8%)
  starting transfers between devices  17.4 us (4%)
    dot_general x16, matrix products, depthwise(): jnp.einsum('cgl,cg->cl', stacked, kernel_taps[:, first:last], preferred_e...  151 us
    unnamed x91, other arithmetic  67.5 us
    unnamed x49, local copies, waits for them, and re-layouts  62 us
    dot_general x18, matrix products, contract(): return jnp.einsum(form, left, right, precision=lax.Precision.HIGHEST)  50 us
    all_to_all x1, waiting for transfers between devices, on_device(): lax.all_to_all(windows, ('tok', 'sec'), split_axis=1, concat_axis=0, tile...  23.6 us
    another operation x8, other arithmetic, depthwise(): jnp.stack([padded[:, tap_count - 1 - k:tap_count - 1 - k + length] for k...  19.8 us
    all_to_all x1, waiting for transfers between devices, on_device(): lax.all_to_all(mixed_one[:, None, :], ('tok', 'sec'), split_axis=0, conca...  10.4 us
  transfers between devices with their start and end apart: 4, of which 2 were waited for; matrix products, arithmetic and copies ran while one was open for 43% of the time, Pallas kernels for 0%

commit v1 on v0

--- a/solution.py
+++ b/solution.py
@@ -106,8 +106,14 @@
         axis=1,
     )
     windows = jnp.concatenate([tail_rows, long_blocks], axis=2)
-    padded = lax.all_to_all(
-        windows, ("tok", "sec"), split_axis=1, concat_axis=0, tiled=True
+    padded = jnp.concatenate(
+        lax.all_to_all(
+            jnp.stack(jnp.split(windows, lax.axis_size(("tok", "sec")), axis=1)),
+            ("tok", "sec"),
+            0,
+            0,
+        ),
+        axis=0,
     ).reshape(channels, block_len + rim_width)
     second_conv = depthwise(padded, taps_two)
     return (second_conv * gate_two).astype(jnp.bfloat16)

time: 436 us -> 441 us (1.011)
  local copies, waits for them, and re-layouts: 78 us -> 83.9 us
    unnamed x49 -> x56, local copies, waits for them, and re-layouts: 62 us -> 66.5 us
  transfers between devices with their start and end apart: 4 -> 4, of which waited for: 2 -> 2; matrix products, arithmetic and copies ran while one was open for 43% -> 42% of each run, Pallas kernels for 0% -> 0%
where the time goes in v1:
time: 441 us; the launch traced here: 434 us
  matrix products  201 us (46%)
  other arithmetic  97.2 us (22%)
  local copies, waits for them, and re-layouts  83.9 us (19%)
  waiting for transfers between devices  34.1 us (8%)
  starting transfers between devices  17.4 us (4%)
    dot_general x16, matrix products, depthwise(): jnp.einsum('cgl,cg->cl', stacked, kernel_taps[:, first:last], preferred_e...  151 us
    unnamed x91, other arithmetic  67.4 us
    unnamed x56, local copies, waits for them, and re-layouts  66.5 us
    dot_general x18, matrix products, contract(): return jnp.einsum(form, left, right, precision=lax.Precision.HIGHEST)  50 us
    all_to_all x1, waiting for transfers between devices, on_device(): lax.all_to_all(jnp.stack(jnp.split(windows, lax.axis_size(('tok', 'sec'))...  23.6 us
    another operation x8, other arithmetic, depthwise(): jnp.stack([padded[:, tap_count - 1 - k:tap_count - 1 - k + length] for k...  19.7 us
    all_to_all x1, waiting for transfers between devices, on_device(): lax.all_to_all(mixed_one[:, None, :], ('tok', 'sec'), split_axis=0, conca...  10.4 us
  transfers between devices with their start and end apart: 4, of which 2 were waited for; matrix products, arithmetic and copies ran while one was open for 42% of the time, Pallas kernels for 0%

profile of v1, /device:TPU:0, one launch (start us, length us, event | category | flops | bytes accessed | tf_op | source)
XLA Modules:
  0.0 434.0 jit_solution(11005912190128471713)
XLA Ops:
  7.9 6.1 %all-to-all-start.1 = ((bf16[8,2,16384]{2,1,0:T(2,128)(2,1)}), bf16[8,2,16384]{2,1,0:T(2,128)(2,1)S(1)}, u32[]{:S(2)}, u32[]{:S(2)}) async-start(bf16[8,2,16384]{2,1,0:T(2,128)(2,1)} %reshape.107), calls=%async_computation.1 | async-start | bytes 1048576 | tf_op jit(solution)/shard_map/all_to_all | solution.py:79
  14.1 5.7 %slice_bitcast_fusion.142 = (bf16[2048,16,1]{1,0,2:T(8,128)(2,1)S(1)}, bf16[2048,16,1]{1,0,2:T(8,128)(2,1)}, bf16[2048,16,1]{1,0,2:T(8,128)(2,1)}, bf16[2048,16,...) fusion(bf16[2048,128]{1,0:T(8,128)(2,1)} %param.9), kind=kLoop, calls=%fused_computation.1021 | loop fusion | bytes 1048576 | tf_op jit(solution)/shard_map/slice | solution.py:26
  27.7 3.2 copy-done.13
  31.0 3.7 constant_dynamic-update-slice_fusion.16
  50.5 3.0 constant_dynamic-update-slice_fusion
  59.8 3.2 constant_dynamic-update-slice_fusion.32
  68.8 2.8 constant_dynamic-update-slice_fusion.48
  110.4 8.7 %fusion.16 = f32[2048,1,128]{2,1,0:T(1,128)S(1)} fusion(bf16[2048,16,128]{2,0,1:T(8,128)(2,1)} %constant_dynamic-update-slice_fusion.112, bf16[2048,16,1]{1,0,2:T(8,128)(2,1)S(1)} %get-tuple-element.199), kind=kOutput, calls=%fused_computation.268 | convolution fusion | flops 8388608 | bytes 9502720 | tf_op jit(solution)/shard_map/cgl,cg->cl/dot_general | solution.py:25
  119.1 8.7 %fusion.18 = f32[2048,1,128]{2,1,0:T(1,128)S(1)} fusion(bf16[2048,16,128]{2,0,1:T(8,128)(2,1)} %get-tuple-element.183, bf16[2048,16,1]{1,0,2:T(8,128)(2,1)S(1)} %get-tuple-element.200), kind=kOutput, calls=%fused_computation.270 | convolution fusion | flops 8388608 | bytes 9502720 | tf_op jit(solution)/shard_map/cgl,cg->cl/dot_general | solution.py:25
  127.8 9.0 %fusion.20 = f32[2048,1,128]{2,1,0:T(1,128)S(1)} fusion(bf16[2048,16,128]{2,0,1:T(8,128)(2,1)} %copy-done.9, bf16[2048,16,1]{1,0,2:T(8,128)(2,1)} %get-tuple-element.194), kind=kOutput, calls=%fused_computation.272 | convolution fusion | flops 8388608 | bytes 9502720 | tf_op jit(solution)/shard_map/cgl,cg->cl/dot_general | solution.py:25
  136.8 9.7 %fusion.22 = f32[2048,1,128]{2,1,0:T(1,128)} fusion(bf16[2048,16,128]{2,0,1:T(8,128)(2,1)} %copy-done.8, bf16[2048,16,1]{1,0,2:T(8,128)(2,1)} %get-tuple-element.195), kind=kOutput, calls=%fused_computation.274 | convolution fusion | flops 8388608 | bytes 9502720 | tf_op jit(solution)/shard_map/cgl,cg->cl/dot_general | solution.py:25
  146.5 10.2 %fusion.24 = f32[2048,1,128]{2,1,0:T(1,128)} fusion(bf16[2048,16,128]{2,0,1:T(8,128)(2,1)} %copy-done.7, bf16[2048,16,1]{1,0,2:T(8,128)(2,1)} %get-tuple-element.196), kind=kOutput, calls=%fused_computation.276 | convolution fusion | flops 8388608 | bytes 9502720 | tf_op jit(solution)/shard_map/cgl,cg->cl/dot_general | solution.py:25
  156.7 9.8 %fusion.26 = f32[2048,1,128]{2,1,0:T(1,128)} fusion(bf16[2048,16,128]{2,0,1:T(8,128)(2,1)} %copy-done.6, bf16[2048,16,1]{1,0,2:T(8,128)(2,1)} %get-tuple-element.197), kind=kOutput, calls=%fused_computation.278 | convolution fusion | flops 8388608 | bytes 9502720 | tf_op jit(solution)/shard_map/cgl,cg->cl/dot_general | solution.py:25
  166.5 9.9 %fusion.30 = f32[2048,1,128]{2,1,0:T(1,128)} fusion(bf16[2048,16,128]{2,0,1:T(8,128)(2,1)} %get-tuple-element.157, bf16[2048,16,1]{1,0,2:T(8,128)(2,1)S(1)} %get-tuple-element.198), kind=kOutput, calls=%fused_computation.282 | convolution fusion | flops 8388608 | bytes 9502720 | tf_op jit(solution)/shard_map/cgl,cg->cl/dot_general | solution.py:25
  176.3 9.8 %fusion.28 = f32[2048,1,128]{2,1,0:T(1,128)} fusion(bf16[2048,16,128]{2,0,1:T(8,128)(2,1)} %get-tuple-element.149, bf16[2048,16,1]{1,0,2:T(8,128)(2,1)S(1)} %get-tuple-element.193), kind=kOutput, calls=%fused_computation.280 | convolution fusion | flops 8388608 | bytes 9502720 | tf_op jit(solution)/shard_map/cgl,cg->cl/dot_general | solution.py:25
  186.1 2.9 fusion.111
  190.9 5.1 %all-to-all-start = ((bf16[8,2,16384]{2,1,0:T(2,128)(2,1)}), bf16[8,2,16384]{2,1,0:T(2,128)(2,1)}, u32[]{:S(2)}, u32[]{:S(2)}) async-start(bf16[8,2,16384]{2,1,0:T(2,128)(2,1)} %reshape.105), calls=%async_computation | async-start | bytes 1048576 | tf_op jit(solution)/shard_map/all_to_all | solution.py:85
  198.6 2.4 fusion.367
  201.0 10.4 %all-to-all-done = bf16[8,2,16384]{2,1,0:T(2,128)(2,1)} async-done(((bf16[8,2,16384]{2,1,0:T(2,128)(2,1)}), bf16[8,2,16384]{2,1,0:T(2,128)(2,1)}, u32[]{:S(2)}, u32[]{:S(2)}) %all-to-all-start) | async-done | bytes 524320 | tf_op jit(solution)/shard_map/all_to_all | solution.py:85
  211.4 2.6 reshape.106
  215.3 3.5 add_bitcast_fusion
  218.8 2.6 fusion.47
  221.4 2.6 fusion.45
  224.0 2.6 fusion.55
  226.6 2.7 fusion.53
  229.4 2.7 fusion.67
  232.1 2.7 fusion.70
  234.8 2.7 fusion.61
  237.5 3.3 multiply_subtract_fusion.1
  240.9 3.6 fusion.34
  244.4 3.6 fusion.32
  248.1 4.0 fusion.73
  252.1 3.8 multiply_subtract_fusion
  258.1 2.6 fusion.91
  268.8 3.7 all-to-all-start.2
  272.5 2.7 slice_bitcast_fusion.134
  275.2 23.6 %all-to-all-done.2 = bf16[8,256,1,255]{3,1,2,0:T(8,128)(2,1)S(1)} async-done(((bf16[8,256,1,255]{3,1,2,0:T(8,128)(2,1)}), bf16[8,256,1,255]{3,1,2,0:T(8,128)(2,1)S(1)}, u32[]{:S(2)}, u32[]{:S(2)}) %all-to-all-start.2) | async-done | bytes 1044512 | tf_op jit(solution)/shard_map/all_to_all | solution.py:110
  298.8 2.7 constant_dynamic-update-slice_fusion.167
  301.6 3.0 constant_dynamic-update-slice_fusion.166
  304.6 3.0 constant_dynamic-update-slice_fusion.165
  307.6 3.0 constant_dynamic-update-slice_fusion.164
  310.6 3.0 constant_dynamic-update-slice_fusion.163
  313.6 3.1 constant_dynamic-update-slice_fusion.162
  316.7 3.0 constant_dynamic-update-slice_fusion.161
  319.7 3.0 constant_dynamic-update-slice_fusion.160
  322.7 3.1 constant_dynamic-update-slice_fusion.159
  325.8 3.2 constant_dynamic-update-slice_fusion.158
  329.0 3.0 constant_dynamic-update-slice_fusion.157
  332.0 3.0 constant_dynamic-update-slice_fusion.156
  335.0 3.0 constant_dynamic-update-slice_fusion.155
  338.0 3.0 constant_dynamic-update-slice_fusion.154
  341.0 3.0 constant_dynamic-update-slice_fusion.153
  344.0 2.8 constant_dynamic-update-slice_fusion.152
  346.8 3.2 copy-done.10
  350.1 2.6 copy-done.11
  355.1 9.1 %fusion.14 = f32[2048,1,128]{2,1,0:T(1,128)S(1)} fusion(bf16[2048,16,128]{2,0,1:T(8,128)(2,1)} %get-tuple-element.20, bf16[2048,16,1]{1,0,2:T(8,128)(2,1)S(1)} %copy-done.5), kind=kOutput, calls=%fused_computation.266 | convolution fusion | flops 8388608 | bytes 9502720 | tf_op jit(solution)/shard_map/cgl,cg->cl/dot_general | solution.py:25
  364.2 8.7 %fusion.12 = f32[2048,1,128]{2,1,0:T(1,128)S(1)} fusion(bf16[2048,16,128]{2,0,1:T(8,128)(2,1)} %copy-done.10, bf16[2048,16,1]{1,0,2:T(8,128)(2,1)S(1)} %copy-done.4), kind=kOutput, calls=%fused_computation.264 | convolution fusion | flops 8388608 | bytes 9502720 | tf_op jit(solution)/shard_map/cgl,cg->cl/dot_general | solution.py:25
  372.9 8.9 %fusion.10 = f32[2048,1,128]{2,1,0:T(1,128)S(1)} fusion(bf16[2048,16,128]{2,0,1:T(8,128)(2,1)} %get-tuple-element.19, bf16[2048,16,1]{1,0,2:T(8,128)(2,1)S(1)} %get-tuple-element.189), kind=kOutput, calls=%fused_computation.262 | convolution fusion | flops 8388608 | bytes 9502720 | tf_op jit(solution)/shard_map/cgl,cg->cl/dot_general | solution.py:25
  381.8 8.8 %fusion.8 = f32[2048,1,128]{2,1,0:T(1,128)S(1)} fusion(bf16[2048,16,128]{2,0,1:T(8,128)(2,1)} %get-tuple-element.18, bf16[2048,16,1]{1,0,2:T(8,128)(2,1)} %get-tuple-element.188), kind=kOutput, calls=%fused_computation.260 | convolution fusion | flops 8388608 | bytes 9502720 | tf_op jit(solution)/shard_map/cgl,cg->cl/dot_general | solution.py:25
  390.6 9.9 %fusion.6 = f32[2048,1,128]{2,1,0:T(1,128)} fusion(bf16[2048,16,128]{2,0,1:T(8,128)(2,1)} %get-tuple-element.17, bf16[2048,16,1]{1,0,2:T(8,128)(2,1)} %get-tuple-element.187), kind=kOutput, calls=%fused_computation.258 | convolution fusion | flops 8388608 | bytes 9502720 | tf_op jit(solution)/shard_map/cgl,cg->cl/dot_general | solution.py:25
  400.5 9.7 %fusion.4 = f32[2048,1,128]{2,1,0:T(1,128)} fusion(bf16[2048,16,128]{2,0,1:T(8,128)(2,1)} %get-tuple-element.16, bf16[2048,16,1]{1,0,2:T(8,128)(2,1)} %get-tuple-element.186), kind=kOutput, calls=%fused_computation.256 | convolution fusion | flops 8388608 | bytes 9502720 | tf_op jit(solution)/shard_map/cgl,cg->cl/dot_general | solution.py:25
  410.3 9.7 %fusion.2 = f32[2048,1,128]{2,1,0:T(1,128)} fusion(bf16[2048,16,128]{2,0,1:T(8,128)(2,1)} %copy-done.12, bf16[2048,16,1]{1,0,2:T(8,128)(2,1)S(1)} %get-tuple-element.192), kind=kOutput, calls=%fused_computation.254 | convolution fusion | flops 8388608 | bytes 9502720 | tf_op jit(solution)/shard_map/cgl,cg->cl/dot_general | solution.py:25
  419.9 10.0 %fusion = f32[2048,1,128]{2,1,0:T(1,128)} fusion(bf16[2048,16,128]{2,0,1:T(8,128)(2,1)} %copy-done.11, bf16[2048,16,1]{1,0,2:T(8,128)(2,1)} %get-tuple-element.191), kind=kOutput, calls=%fused_computation.252 | convolution fusion | flops 8388608 | bytes 9502720 | tf_op jit(solution)/shard_map/cgl,cg->cl/dot_general | solution.py:25
  430.0 3.6 multiply_convert_fusion
  (148 shorter events, 100.8 us)
Async XLA Ops:
  0.0 19.8 %copy-start = (bf16[2048,128]{1,0:T(8,128)(2,1)S(1)}, bf16[2048,128]{1,0:T(8,128)(2,1)}, u32[]{:S(2)}) copy-start(bf16[2048,128]{1,0:T(8,128)(2,1)} %param.7) | copy-start | bytes 1572868
  2.1 17.6 %collective-permute-start = (bf16[2048,127]{1,0:T(8,128)(2,1)}, bf16[2048,127]{1,0:T(8,128)(2,1)S(1)}, u32[]{:S(2)}, u32[]{:S(2)}) collective-permute-start(bf16[2048,127]{1,0:T(8,128)(2,1)} %slice.819), channel_id=1, source_target_pairs={{0,2},{2,4},{4,6},{6,8},{8,10},{10,12},{12,14},{1,3},{3,5},{5,7},{... | collective-permute-start | bytes 1560584 | tf_op jit(solution)/shard_map/ppermute | solution.py:11
  7.9 183.0 %all-to-all-start.1 = ((bf16[8,2,16384]{2,1,0:T(2,128)(2,1)}), bf16[8,2,16384]{2,1,0:T(2,128)(2,1)S(1)}, u32[]{:S(2)}, u32[]{:S(2)}) async-start(bf16[8,2,16384]{2,1,0:T(2,128)(2,1)} %reshape.107), calls=%async_computation.1 | async-start | bytes 1048576 | tf_op jit(solution)/shard_map/all_to_all | solution.py:79
  27.7 3.2 copy-start.13
  63.0 5.3 %copy-start.6 = (bf16[2048,16,128]{2,0,1:T(8,128)(2,1)}, bf16[2048,16,128]{2,0,1:T(8,128)(2,1)S(1)}, u32[]{:S(2)}) copy-start(bf16[2048,16,128]{2,0,1:T(8,128)(2,1)S(1)} %get-tuple-element.165) | copy-start | bytes 25165828
  71.6 5.3 %copy-start.7 = (bf16[2048,16,128]{2,0,1:T(8,128)(2,1)}, bf16[2048,16,128]{2,0,1:T(8,128)(2,1)S(1)}, u32[]{:S(2)}) copy-start(bf16[2048,16,128]{2,0,1:T(8,128)(2,1)S(1)} %get-tuple-element.171) | copy-start | bytes 25165828
  79.2 7.1 %copy-start.8 = (bf16[2048,16,128]{2,0,1:T(8,128)(2,1)}, bf16[2048,16,128]{2,0,1:T(8,128)(2,1)S(1)}, u32[]{:S(2)}) copy-start(bf16[2048,16,128]{2,0,1:T(8,128)(2,1)S(1)} %get-tuple-element.176) | copy-start | bytes 25165828
  86.4 14.3 %copy-start.9 = (bf16[2048,16,128]{2,0,1:T(8,128)(2,1)}, bf16[2048,16,128]{2,0,1:T(8,128)(2,1)S(1)}, u32[]{:S(2)}) copy-start(bf16[2048,16,128]{2,0,1:T(8,128)(2,1)S(1)} %get-tuple-element.180) | copy-start | bytes 25165828
  176.3 9.8 %copy-start.2 = (bf16[2048,128]{1,0:T(8,128)(2,1)S(1)}, bf16[2048,128]{1,0:T(8,128)(2,1)}, u32[]{:S(2)}) copy-start(bf16[2048,128]{1,0:T(8,128)(2,1)} %param.8) | copy-start | bytes 1572868
  190.9 20.5 %all-to-all-start = ((bf16[8,2,16384]{2,1,0:T(2,128)(2,1)}), bf16[8,2,16384]{2,1,0:T(2,128)(2,1)}, u32[]{:S(2)}, u32[]{:S(2)}) async-start(bf16[8,2,16384]{2,1,0:T(2,128)(2,1)} %reshape.105), calls=%async_computation | async-start | bytes 1048576 | tf_op jit(solution)/shard_map/all_to_all | solution.py:85
  258.1 14.5 %copy-start.1 = (bf16[2048,128]{1,0:T(8,128)(2,1)S(1)}, bf16[2048,128]{1,0:T(8,128)(2,1)}, u32[]{:S(2)}) copy-start(bf16[2048,128]{1,0:T(8,128)(2,1)} %param.12) | copy-start | bytes 1572868
  268.8 30.1 %all-to-all-start.2 = ((bf16[8,256,1,255]{3,1,2,0:T(8,128)(2,1)}), bf16[8,256,1,255]{3,1,2,0:T(8,128)(2,1)S(1)}, u32[]{:S(2)}, u32[]{:S(2)}) async-start(bf16[8,256,1,255]{3,1,2,0:T(8,128)(2,1)} %constant_dynamic-update-slice_fusion.128), calls=%async_computation.2 | async-start | bytes 2097152 | tf_op jit(solution)/shard_map/all_to_all | solution.py:110
  341.0 14.1 %copy-start.5 = (bf16[2048,16,1]{1,0,2:T(8,128)(2,1)S(1)}, bf16[2048,16,1]{1,0,2:T(8,128)(2,1)}, u32[]{:S(2)}) copy-start(bf16[2048,16,1]{1,0,2:T(8,128)(2,1)} %get-tuple-element.190) | copy-start | bytes 196612
  346.8 3.2 copy-start.10
  346.8 5.8 %copy-start.11 = (bf16[2048,16,128]{2,0,1:T(8,128)(2,1)}, bf16[2048,16,128]{2,0,1:T(8,128)(2,1)S(1)}, u32[]{:S(2)}) copy-start(bf16[2048,16,128]{2,0,1:T(8,128)(2,1)S(1)} %get-tuple-element.14) | copy-start | bytes 25165828
  346.8 8.3 %copy-start.12 = (bf16[2048,16,128]{2,0,1:T(8,128)(2,1)}, bf16[2048,16,128]{2,0,1:T(8,128)(2,1)S(1)}, u32[]{:S(2)}) copy-start(bf16[2048,16,128]{2,0,1:T(8,128)(2,1)S(1)} %get-tuple-element.15) | copy-start | bytes 25165828
  346.8 17.4 %copy-start.4 = (bf16[2048,16,1]{1,0,2:T(8,128)(2,1)S(1)}, bf16[2048,16,1]{1,0,2:T(8,128)(2,1)}, u32[]{:S(2)}) copy-start(bf16[2048,16,1]{1,0,2:T(8,128)(2,1)} %get-tuple-element.185) | copy-start | bytes 196612
  419.9 10.1 %copy-start.3 = (bf16[2048,128]{1,0:T(8,128)(2,1)S(1)}, bf16[2048,128]{1,0:T(8,128)(2,1)}, u32[]{:S(2)}) copy-start(bf16[2048,128]{1,0:T(8,128)(2,1)} %param.13) | copy-start | bytes 1572868
